TPU v7x, 32 devices: a whole 2x2x4 slice. The times are simulated.
32 devices in a mesh: groups: 2 (over y), ctx: 4 (over z), mp: 4 (over x, core).
Axes of the slice: x: 2, y: 2, z: 4, core: 2. Of those that a mesh axis runs over, the one named last changes fastest.
Arguments:
- queries: bfloat16 [2048, 4096], P(('groups', 'ctx'), 'mp'), parts along dimension 0, may hold values from -18 to 18
- keyvals: bfloat16 [2048, 512], P(('groups', 'ctx', 'mp')), parts along dimension 0, may hold values from -6 to 6
- segment_ids: int32 [2048], P('groups'), parts along dimension 0, may hold values from 0 to 2, never falling along the last dimension, each value on 1 to 512 neighbouring positions
- residual: bfloat16 [2048, 4096], P(('groups', 'ctx', 'mp')), parts along dimension 0, may hold values from -180 to 180
- out_weight: bfloat16 [4096, 4096], P('mp', 'ctx'), may hold values from -0.375 to 0.375
- lru_weight: bfloat16 [4096, 4096], P('ctx', 'mp'), may hold values from -0.09375 to 0.09375
- conv_weight: float32 [4, 4096], P(None, 'mp'), may hold values from -3 to 3
- gate_decay_w: bfloat16 [16, 256, 256], P('mp'), may hold values from -0.375 to 0.375
- gate_input_w: bfloat16 [16, 256, 256], P('mp'), may hold values from -0.375 to 0.375
- gate_decay_b: float32 [4096], P('mp'), may hold values from -3 to 3
- gate_input_b: float32 [4096], P('mp'), may hold values from -3 to 3
- decay_codes: int32 [4096], P('mp'), may hold values from 0 to 15
- norm_gain: float32 [4096], replicated, may hold values from 0.1 to 1.9
Outputs:
- resid_out: bfloat16 [2048, 4096], P(('groups', 'ctx', 'mp')), parts along dimension 0
- lru_out: bfloat16 [2048, 4096], P(('groups', 'ctx'), 'mp'), parts along dimension 0
There are 2 independent parts, one for each index of `groups`. A program takes and returns all parts, laid end to end along the dimension named above; an argument that names none is the same for every part. Nothing has to cross between parts.
All inputs are finite; a program needn't handle non-finite values.
Results may differ from a plain program's by a relative error of at most 0.017.
Values may be sent and summed in bfloat16 or wider, within the bound.
No kernel may reach another device: no remote copies, remote signals or barrier semaphores. Data moves between devices by JAX's collectives and lax.ppermute only.
A program may use at most 64 MiB of HBM per device.

v0:
```python
import math
import jax
import jax.numpy as jnp
from jax import lax
from jax.sharding import PartitionSpec as P

HD = 256
WIN = 2048
CONV = 4
LEVELS = 16
BW = 256


def shifted_2(value, axis, steps):
    count = lax.axis_size(axis)
    initial, last = (max(0, -steps), min(count, count - steps))
    return lax.ppermute(value, axis, [(source, source + steps) for source in range(initial, last)])


def decay_rates():
    levels = jnp.arange(LEVELS, dtype=jnp.float32)
    return 0.006 * jnp.exp(-levels * (math.log(3000.0) / (LEVELS - 1)))


def chain_link(former, latter):
    return (former[0] * latter[0], latter[0] * former[1] + latter[1])


def rms_scaled(values, norm_gain):
    value_f32 = values.astype(jnp.float32)
    inverse = lax.rsqrt(jnp.mean(value_f32 * value_f32, axis=-1, keepdims=True) + 1e-06)
    return (value_f32 * inverse * norm_gain).astype(jnp.bfloat16)


def attend_local(queries, keys_all, allowed):
    rows_here = queries.shape[0]
    heads_here = queries.shape[1] // HD
    query_heads = queries.reshape(rows_here, heads_here, HD)
    score_scale = 1.0 / math.sqrt(HD)
    scores = (
        jnp.einsum("thd,kd->htk", query_heads, keys_all[:, :HD], preferred_element_type=jnp.float32)
        * score_scale
    )
    scores = jnp.where(allowed[None], scores, -1e30)
    row_top = jnp.max(scores, axis=-1, keepdims=True)
    weights = jnp.exp(scores - row_top)
    probs = (weights / jnp.sum(weights, axis=-1, keepdims=True)).astype(jnp.bfloat16)
    gathered = jnp.einsum(
        "htk,kd->thd", probs, keys_all[:, HD:], preferred_element_type=jnp.float32
    )
    return gathered.reshape(rows_here, heads_here * HD).astype(jnp.bfloat16)


def local(
    queries,
    keyvals,
    segment_ids,
    residual,
    out_weight,
    lru_weight,
    conv_weight,
    gate_decay_w,
    gate_input_w,
    gate_decay_b,
    gate_input_b,
    decay_codes,
    norm_gain,
):
    rows_here = queries.shape[0]
    ctx_index = lax.axis_index("ctx")
    back_blocks = WIN // rows_here
    own_kv = lax.all_gather(keyvals, "mp", axis=0, tiled=True)
    earlier = []
    moving = own_kv
    for offset in range(back_blocks):
        moving = shifted_2(moving, "ctx", 1)
        earlier = [moving] + earlier
    keys_all = jnp.concatenate(earlier + [own_kv], axis=0)
    pad_seg = jnp.concatenate([jnp.full((WIN,), -1, jnp.int32), segment_ids])
    query_seg = lax.dynamic_slice_in_dim(segment_ids, ctx_index * rows_here, rows_here)
    key_seg = lax.dynamic_slice_in_dim(
        pad_seg, ctx_index * rows_here, (back_blocks + 1) * rows_here
    )
    query_pos = ctx_index * rows_here + jnp.arange(rows_here, dtype=jnp.int32)
    key_pos = (ctx_index - back_blocks) * rows_here + jnp.arange(
        (back_blocks + 1) * rows_here, dtype=jnp.int32
    )
    distance = query_pos[:, None] - key_pos[None, :]
    allowed = (distance >= 0) & (distance < WIN) & (query_seg[:, None] == key_seg[None, :])
    attended = attend_local(queries, keys_all, allowed)
    head_part = jnp.dot(
        attended,
        lax.all_gather(out_weight, "ctx", axis=1, tiled=True),
        preferred_element_type=jnp.float32,
    )
    summed = lax.psum_scatter(
        head_part.astype(jnp.bfloat16), "mp", scatter_dimension=0, tiled=True
    ).astype(jnp.float32)
    resid_out = (summed + residual.astype(jnp.float32)).astype(jnp.bfloat16)
    normed = lax.all_gather(rms_scaled(resid_out, norm_gain), "mp", axis=0, tiled=True)
    channels = lru_weight.shape[1]
    lru_in = jnp.dot(
        normed,
        lax.all_gather(lru_weight, "ctx", axis=0, tiled=True),
        preferred_element_type=jnp.float32,
    ).astype(jnp.bfloat16)
    rim_rows = shifted_2(lru_in[rows_here - (CONV - 1) :], "ctx", 1)
    extended = jnp.concatenate([rim_rows, lru_in], axis=0)
    ext_seg = lax.dynamic_slice_in_dim(
        pad_seg, ctx_index * rows_here + WIN - (CONV - 1), rows_here + CONV - 1
    )
    conv_acc = jnp.zeros((rows_here, channels), jnp.float32)
    for offset in range(CONV):
        lag_rows = CONV - 1 - offset
        shifted = extended[lag_rows : lag_rows + rows_here].astype(jnp.float32)
        same_doc = (ext_seg[lag_rows : lag_rows + rows_here] == query_seg)[:, None]
        conv_acc = conv_acc + jnp.where(same_doc, conv_weight[offset] * shifted, 0.0)
    conv_out = conv_acc.astype(jnp.bfloat16)
    blocks_here = channels // BW
    grouped = conv_out.reshape(rows_here, blocks_here, BW)
    decay_gate = jax.nn.sigmoid(
        jnp.einsum(
            "tbi,bij->tbj", grouped, gate_decay_w, preferred_element_type=jnp.float32
        ).reshape(rows_here, channels)
        + gate_decay_b
    )
    input_gate = jax.nn.sigmoid(
        jnp.einsum(
            "tbi,bij->tbj", grouped, gate_input_w, preferred_element_type=jnp.float32
        ).reshape(rows_here, channels)
        + gate_input_b
    )
    levels = jnp.arange(LEVELS, dtype=jnp.int32)
    decay_rate = jnp.sum(
        jnp.where(decay_codes[:, None] == levels[None, :], decay_rates()[None, :], 0.0), axis=1
    )
    log_decay = -8.0 * decay_gate * decay_rate
    restart = (query_seg != ext_seg[CONV - 2 : CONV - 2 + rows_here])[:, None]
    keep_factor = jnp.where(restart, 0.0, jnp.exp(log_decay))
    input_scale = jnp.where(restart, 1.0, jnp.sqrt(-jnp.expm1(2.0 * log_decay)))
    driven = input_scale * input_gate * conv_out.astype(jnp.float32)
    cum_keep, local_state = lax.associative_scan(chain_link, (keep_factor, driven), axis=0)
    block_keep = cum_keep[rows_here - 1]
    block_state = local_state[rows_here - 1]

    def relay_turn(turn_index, state_in):
        return shifted_2(block_keep * state_in + block_state, "ctx", 1)

    incoming = lax.fori_loop(0, lax.axis_size("ctx") - 1, relay_turn, jnp.zeros_like(block_state))
    states = local_state + cum_keep * incoming[None, :]
    return (resid_out, states.astype(jnp.bfloat16))


def solution(mesh):
    in_specs = (
        P(("groups", "ctx"), "mp"),
        P(("groups", "ctx", "mp"), None),
        P("groups"),
        P(("groups", "ctx", "mp"), None),
        P("mp", "ctx"),
        P("ctx", "mp"),
        P(None, "mp"),
        P("mp", None, None),
        P("mp", None, None),
        P("mp"),
        P("mp"),
        P("mp"),
        P(),
    )
    out_specs = (P(("groups", "ctx", "mp"), None), P(("groups", "ctx"), "mp"))
    return jax.shard_map(local, mesh=mesh, in_specs=in_specs, out_specs=out_specs, check_vma=False)
```

profile of v0, /device:TPU:0, one launch (start us, length us, event | category | flops | bytes accessed | tf_op | source)
XLA Modules:
  0.0 554.3 jit_solution(5232723126797398906)
XLA Ops:
  8.0 7.4 %all_gather.12 = bf16[256,512]{1,0:T(8,128)(2,1)S(1)} all-gather(bf16[64,512]{1,0:T(8,128)(2,1)} %param.16), channel_id=1, replica_groups=mesh['groups'=2,'ctx'=4,'mp'=4] {'mp'}, dimensions={0}, use_global_device_ids=true | all-gather | bytes 327680 | tf_op jit(solution)/shard_map/all_gather | solution.py:72
  15.4 3.5 collective-permute-start.1
  18.9 9.3 %collective-permute-done.1 = bf16[256,512]{1,0:T(8,128)(2,1)S(1)} collective-permute-done((bf16[256,512]{1,0:T(8,128)(2,1)S(1)}, bf16[256,512]{1,0:T(8,128)(2,1)S(1)}, u32[]{:S(2)}, u32[]{:S(2)}) %collective-permute-start.1) | collective-permute-done | bytes 262176 | tf_op jit(solution)/shard_map/ppermute | solution.py:17
  28.3 8.5 %collective-permute-start.2 = (bf16[256,512]{1,0:T(8,128)(2,1)S(1)}, bf16[256,512]{1,0:T(8,128)(2,1)S(1)}, u32[]{:S(2)}, u32[]{:S(2)}) collective-permute-start(bf16[256,512]{1,0:T(8,128)(2,1)S(1)} %collective-permute-done.1), channel_id=1, source_target_pairs={{0,4},{4,8},{8,12},{1,5},{5,9},{9,13},{2,6},{6,10},{10,14},{3,7},{... | collective-permute-start | bytes 786440 | tf_op jit(solution)/shard_map/ppermute | solution.py:17
  36.8 11.2 %collective-permute-done.2 = bf16[256,512]{1,0:T(8,128)(2,1)S(1)} collective-permute-done((bf16[256,512]{1,0:T(8,128)(2,1)S(1)}, bf16[256,512]{1,0:T(8,128)(2,1)S(1)}, u32[]{:S(2)}, u32[]{:S(2)}) %collective-permute-start.2) | collective-permute-done | bytes 262176 | tf_op jit(solution)/shard_map/ppermute | solution.py:17
  48.0 13.6 %collective-permute-start.3 = (bf16[256,512]{1,0:T(8,128)(2,1)S(1)}, bf16[256,512]{1,0:T(8,128)(2,1)S(1)}, u32[]{:S(2)}, u32[]{:S(2)}) collective-permute-start(bf16[256,512]{1,0:T(8,128)(2,1)S(1)} %collective-permute-done.2), channel_id=1, source_target_pairs={{0,4},{4,8},{8,12},{1,5},{5,9},{9,13},{2,6},{6,10},{10,14},{3,7},{... | collective-permute-start | bytes 786440 | tf_op jit(solution)/shard_map/ppermute | solution.py:17
  61.6 10.2 %collective-permute-done.3 = bf16[256,512]{1,0:T(8,128)(2,1)S(1)} collective-permute-done((bf16[256,512]{1,0:T(8,128)(2,1)S(1)}, bf16[256,512]{1,0:T(8,128)(2,1)S(1)}, u32[]{:S(2)}, u32[]{:S(2)}) %collective-permute-start.3) | collective-permute-done | bytes 262176 | tf_op jit(solution)/shard_map/ppermute | solution.py:17
  71.8 12.3 %collective-permute-start.4 = (bf16[256,512]{1,0:T(8,128)(2,1)S(1)}, bf16[256,512]{1,0:T(8,128)(2,1)S(1)}, u32[]{:S(2)}, u32[]{:S(2)}) collective-permute-start(bf16[256,512]{1,0:T(8,128)(2,1)S(1)} %collective-permute-done.3), channel_id=1, source_target_pairs={{0,4},{4,8},{8,12},{1,5},{5,9},{9,13},{2,6},{6,10},{10,14},{3,7},{... | collective-permute-start | bytes 786440 | tf_op jit(solution)/shard_map/ppermute | solution.py:17
  84.1 9.6 %collective-permute-done.4 = bf16[256,512]{1,0:T(8,128)(2,1)S(1)} collective-permute-done((bf16[256,512]{1,0:T(8,128)(2,1)S(1)}, bf16[256,512]{1,0:T(8,128)(2,1)S(1)}, u32[]{:S(2)}, u32[]{:S(2)}) %collective-permute-start.4) | collective-permute-done | bytes 262176 | tf_op jit(solution)/shard_map/ppermute | solution.py:17
  93.7 11.3 %collective-permute-start.5 = (bf16[256,512]{1,0:T(8,128)(2,1)S(1)}, bf16[256,512]{1,0:T(8,128)(2,1)S(1)}, u32[]{:S(2)}, u32[]{:S(2)}) collective-permute-start(bf16[256,512]{1,0:T(8,128)(2,1)S(1)} %collective-permute-done.4), channel_id=1, source_target_pairs={{0,4},{4,8},{8,12},{1,5},{5,9},{9,13},{2,6},{6,10},{10,14},{3,7},{... | collective-permute-start | bytes 786440 | tf_op jit(solution)/shard_map/ppermute | solution.py:17
  105.0 9.7 %collective-permute-done.5 = bf16[256,512]{1,0:T(8,128)(2,1)S(1)} collective-permute-done((bf16[256,512]{1,0:T(8,128)(2,1)S(1)}, bf16[256,512]{1,0:T(8,128)(2,1)S(1)}, u32[]{:S(2)}, u32[]{:S(2)}) %collective-permute-start.5) | collective-permute-done | bytes 262176 | tf_op jit(solution)/shard_map/ppermute | solution.py:17
  114.6 13.8 %collective-permute-start.6 = (bf16[256,512]{1,0:T(8,128)(2,1)S(1)}, bf16[256,512]{1,0:T(8,128)(2,1)S(1)}, u32[]{:S(2)}, u32[]{:S(2)}) collective-permute-start(bf16[256,512]{1,0:T(8,128)(2,1)S(1)} %collective-permute-done.5), channel_id=1, source_target_pairs={{0,4},{4,8},{8,12},{1,5},{5,9},{9,13},{2,6},{6,10},{10,14},{3,7},{... | collective-permute-start | bytes 786440 | tf_op jit(solution)/shard_map/ppermute | solution.py:17
  128.7 9.4 %collective-permute-done.6 = bf16[256,512]{1,0:T(8,128)(2,1)S(1)} collective-permute-done((bf16[256,512]{1,0:T(8,128)(2,1)S(1)}, bf16[256,512]{1,0:T(8,128)(2,1)S(1)}, u32[]{:S(2)}, u32[]{:S(2)}) %collective-permute-start.6) | collective-permute-done | bytes 262176 | tf_op jit(solution)/shard_map/ppermute | solution.py:17
  138.1 9.9 %collective-permute-start.7 = (bf16[256,512]{1,0:T(8,128)(2,1)S(1)}, bf16[256,512]{1,0:T(8,128)(2,1)S(1)}, u32[]{:S(2)}, u32[]{:S(2)}) collective-permute-start(bf16[256,512]{1,0:T(8,128)(2,1)S(1)} %collective-permute-done.6), channel_id=1, source_target_pairs={{0,4},{4,8},{8,12},{1,5},{5,9},{9,13},{2,6},{6,10},{10,14},{3,7},{... | collective-permute-start | bytes 786440 | tf_op jit(solution)/shard_map/ppermute | solution.py:17
  148.1 9.5 %collective-permute-done.7 = bf16[256,512]{1,0:T(8,128)(2,1)S(1)} collective-permute-done((bf16[256,512]{1,0:T(8,128)(2,1)S(1)}, bf16[256,512]{1,0:T(8,128)(2,1)S(1)}, u32[]{:S(2)}, u32[]{:S(2)}) %collective-permute-start.7) | collective-permute-done | bytes 262176 | tf_op jit(solution)/shard_map/ppermute | solution.py:17
  157.6 13.0 %collective-permute-start.8 = (bf16[256,512]{1,0:T(8,128)(2,1)S(1)}, bf16[256,512]{1,0:T(8,128)(2,1)S(1)}, u32[]{:S(2)}, u32[]{:S(2)}) collective-permute-start(bf16[256,512]{1,0:T(8,128)(2,1)S(1)} %collective-permute-done.7), channel_id=1, source_target_pairs={{0,4},{4,8},{8,12},{1,5},{5,9},{9,13},{2,6},{6,10},{10,14},{3,7},{... | collective-permute-start | bytes 786440 | tf_op jit(solution)/shard_map/ppermute | solution.py:17
  170.6 1.6 fusion.7
  172.2 8.0 %collective-permute-done.8 = bf16[256,512]{1,0:T(8,128)(2,1)S(1)} collective-permute-done((bf16[256,512]{1,0:T(8,128)(2,1)S(1)}, bf16[256,512]{1,0:T(8,128)(2,1)S(1)}, u32[]{:S(2)}, u32[]{:S(2)}) %collective-permute-start.8) | collective-permute-done | bytes 262176 | tf_op jit(solution)/shard_map/ppermute | solution.py:17
  180.4 1.4 copy-done.12
  181.8 4.7 fusion.53
  186.5 6.0 %fusion.8 = bf16[256,4,256]{2,0,1:T(8,128)(2,1)S(1)} fusion(f32[4,256]{1,0:T(4,128)S(1)} %fusion.53, bf16[2304,512]{1,0:T(8,128)(2,1)} %copy-done.12, pred[256,2304]{0,1:T(8,128)(4,1)S(1)} %fusion.7, bf16[32,4,8,256]{3,2,1,0:T(8,128)(2,1)S(1)} %bitcast.79), kind=kOutput, calls=%fused_computation.17 | convolution fusion | flops 2427981056 | bytes 4001792 | tf_op jit(solution)/shard_map/htk,kd->thd/dot_general | solution.py:48
  192.5 6.9 %all-gather.4.cloned.1.call-done = bf16[1024,4096]{1,0:T(8,128)(2,1)} async-done(((bf16[1024,1024]{1,0:T(8,128)(2,1)}), bf16[1024,4096]{1,0:T(8,128)(2,1)}) %all-gather.4.cloned.1.call-update) | async-done | bytes 8388624 | tf_op jit(solution)/shard_map/all_gather | solution.py:93
  199.5 7.1 %convolution_convert_fusion = bf16[256,4096]{1,0:T(8,128)(2,1)} fusion(bf16[256,1024]{0,1:T(8,128)(2,1)S(1)} %bitcast.71, bf16[1024,4096]{1,0:T(8,128)(2,1)} %all-gather.4.cloned.1.call-done), kind=kOutput, calls=%fused_computation.6 | convolution fusion | flops 2148532224 | bytes 11010048 | tf_op jit(solution)/shard_map/dot_general | solution.py:91
  207.6 33.9 %reduce-scatter.2.cloned.1.call-done = bf16[64,4096]{1,0:T(8,128)(2,1)} async-done(((bf16[256,4096]{1,0:T(8,128)(2,1)}), bf16[64,4096]{1,0:T(8,128)(2,1)}) %reduce-scatter.2.cloned.1.call-update) | async-done | bytes 524304 | tf_op jit(solution)/shard_map/reduce_scatter | solution.py:96
  244.8 147.9 %all-gather.8.cloned.1.call-done = bf16[4096,1024]{1,0:T(8,128)(2,1)} async-done(((bf16[1024,1024]{1,0:T(8,128)(2,1)}), bf16[4096,1024]{1,0:T(8,128)(2,1)}) %all-gather.8.cloned.1.call-update) | async-done | bytes 8388624 | tf_op jit(solution)/shard_map/all_gather | solution.py:104
  392.8 22.8 %all-gather.6.cloned.1.call-done = bf16[256,4096]{1,0:T(8,128)(2,1)} async-done(((bf16[64,4096]{1,0:T(8,128)(2,1)}), bf16[256,4096]{1,0:T(8,128)(2,1)}) %all-gather.6.cloned.1.call-update) | async-done | bytes 2097168 | tf_op jit(solution)/shard_map/all_gather | solution.py:100
  415.5 6.3 %convolution_convert_fusion.1 = bf16[256,1024]{1,0:T(8,128)(2,1)S(1)} fusion(bf16[256,4096]{1,0:T(8,128)(2,1)} %all-gather.6.cloned.1.call-done, bf16[4096,1024]{1,0:T(8,128)(2,1)} %all-gather.8.cloned.1.call-done), kind=kOutput, calls=%fused_computation.18 | convolution fusion | flops 2147745792 | bytes 11010048 | tf_op jit(solution)/shard_map/dot_general | solution.py:102
  421.9 3.4 collective-permute-start.9
  430.8 2.8 convert_multiply_fusion.2
  433.6 1.4 slice.296
  435.0 1.5 slice.297
  436.5 1.5 slice.295
  438.0 1.5 slice.299
  439.4 2.5 multiply_add_fusion.1
  441.9 1.7 slice.302
  443.6 1.7 slice.303
  446.8 1.9 multiply_add_fusion.2
  450.1 1.6 slice.307
  451.7 1.6 slice.311
  453.4 1.8 multiply_add_fusion.3
  456.4 1.5 slice.313
  457.9 1.5 slice.317
  459.5 1.6 multiply_add_fusion.4
  461.0 1.4 slice.320
  462.5 1.4 slice.321
  463.9 1.4 slice.319
  465.4 1.5 slice.323
  466.8 1.4 multiply_add_fusion.5
  480.4 1.4 fusion.50
  487.2 1.5 slice.318
  488.7 1.4 slice.343
  492.8 1.5 slice.312
  500.8 1.7 slice.349
  504.5 1.5 slice.294
  506.0 1.5 slice.351
  515.7 2.7 pad.114
  518.6 2.3 fusion.24
  521.1 2.7 pad.130
  525.0 2.7 pad.129
  528.5 16.5 %while.10 = (s32[]{:T(128)}, f32[1024]{0:T(1024)S(1)}, f32[1024]{0:T(1024)S(1)}, f32[1024]{0:T(1024)S(1)}, s32[]{:T(128)}) while((s32[]{:T(128)}, f32[1024]{0:T(1024)S(1)}, f32[1024]{0:T(1024)S(1)}, f32[1024]{0:T(1024)S(1)}, s32[]{:T(128)}) %tuple.63), condition=%wide.region_6.7_spmd, body=%wide.region_5.6_spmd.sunk | while | flops 2050 | bytes 32869 | solution.py:149
  528.5 4.2 collective-permute-start
  534.0 4.2 collective-permute-start
  539.5 4.2 collective-permute-start
  545.0 2.8 add_convert_fusion
  (195 shorter events, 57.5 us)
Async XLA Ops:
  7.2 420.2 %copy-start = (bf16[4,256,256]{2,1,0:T(8,128)(2,1)S(1)}, bf16[4,256,256]{2,1,0:T(8,128)(2,1)}, u32[]{:S(2)}) copy-start(bf16[4,256,256]{2,1,0:T(8,128)(2,1)} %param.22) | copy-start | bytes 1572868
  7.2 121.3 %copy-start.13 = (s32[1024]{0:T(1024)S(1)}, s32[1024]{0:T(1024)}, u32[]{:S(2)}) copy-start(s32[1024]{0:T(1024)} %param.17) | copy-start | bytes 12292
  7.2 192.3 %all-gather.4.cloned.1.call-start = ((), (), s32[]{:S(2)}) async-start(), calls=%async_computation.1 | async-start | bytes 10485760 | tf_op jit(solution)/shard_map/all_gather | solution.py:93
  7.9 233.6 %reduce-scatter.2.cloned.1.call-start = ((), (), s32[]{:S(2)}) async-start(), calls=%async_computation.2 | async-start | bytes 2621440 | tf_op jit(solution)/shard_map/reduce_scatter | solution.py:96
  15.4 12.9 %collective-permute-start.1 = (bf16[256,512]{1,0:T(8,128)(2,1)S(1)}, bf16[256,512]{1,0:T(8,128)(2,1)S(1)}, u32[]{:S(2)}, u32[]{:S(2)}) collective-permute-start(bf16[256,512]{1,0:T(8,128)(2,1)S(1)} %all_gather.12), channel_id=1, source_target_pairs={{0,4},{4,8},{8,12},{1,5},{5,9},{9,13},{2,6},{6,10},{10,14},{3,7},{... | collective-permute-start | bytes 786440 | tf_op jit(solution)/shard_map/ppermute | solution.py:17
  28.3 19.7 %collective-permute-start.2 = (bf16[256,512]{1,0:T(8,128)(2,1)S(1)}, bf16[256,512]{1,0:T(8,128)(2,1)S(1)}, u32[]{:S(2)}, u32[]{:S(2)}) collective-permute-start(bf16[256,512]{1,0:T(8,128)(2,1)S(1)} %collective-permute-done.1), channel_id=1, source_target_pairs={{0,4},{4,8},{8,12},{1,5},{5,9},{9,13},{2,6},{6,10},{10,14},{3,7},{... | collective-permute-start | bytes 786440 | tf_op jit(solution)/shard_map/ppermute | solution.py:17
  48.0 23.8 %collective-permute-start.3 = (bf16[256,512]{1,0:T(8,128)(2,1)S(1)}, bf16[256,512]{1,0:T(8,128)(2,1)S(1)}, u32[]{:S(2)}, u32[]{:S(2)}) collective-permute-start(bf16[256,512]{1,0:T(8,128)(2,1)S(1)} %collective-permute-done.2), channel_id=1, source_target_pairs={{0,4},{4,8},{8,12},{1,5},{5,9},{9,13},{2,6},{6,10},{10,14},{3,7},{... | collective-permute-start | bytes 786440 | tf_op jit(solution)/shard_map/ppermute | solution.py:17
  71.8 21.9 %collective-permute-start.4 = (bf16[256,512]{1,0:T(8,128)(2,1)S(1)}, bf16[256,512]{1,0:T(8,128)(2,1)S(1)}, u32[]{:S(2)}, u32[]{:S(2)}) collective-permute-start(bf16[256,512]{1,0:T(8,128)(2,1)S(1)} %collective-permute-done.3), channel_id=1, source_target_pairs={{0,4},{4,8},{8,12},{1,5},{5,9},{9,13},{2,6},{6,10},{10,14},{3,7},{... | collective-permute-start | bytes 786440 | tf_op jit(solution)/shard_map/ppermute | solution.py:17
  93.7 21.0 %collective-permute-start.5 = (bf16[256,512]{1,0:T(8,128)(2,1)S(1)}, bf16[256,512]{1,0:T(8,128)(2,1)S(1)}, u32[]{:S(2)}, u32[]{:S(2)}) collective-permute-start(bf16[256,512]{1,0:T(8,128)(2,1)S(1)} %collective-permute-done.4), channel_id=1, source_target_pairs={{0,4},{4,8},{8,12},{1,5},{5,9},{9,13},{2,6},{6,10},{10,14},{3,7},{... | collective-permute-start | bytes 786440 | tf_op jit(solution)/shard_map/ppermute | solution.py:17
  114.6 23.4 %collective-permute-start.6 = (bf16[256,512]{1,0:T(8,128)(2,1)S(1)}, bf16[256,512]{1,0:T(8,128)(2,1)S(1)}, u32[]{:S(2)}, u32[]{:S(2)}) collective-permute-start(bf16[256,512]{1,0:T(8,128)(2,1)S(1)} %collective-permute-done.5), channel_id=1, source_target_pairs={{0,4},{4,8},{8,12},{1,5},{5,9},{9,13},{2,6},{6,10},{10,14},{3,7},{... | collective-permute-start | bytes 786440 | tf_op jit(solution)/shard_map/ppermute | solution.py:17
  138.1 19.5 %collective-permute-start.7 = (bf16[256,512]{1,0:T(8,128)(2,1)S(1)}, bf16[256,512]{1,0:T(8,128)(2,1)S(1)}, u32[]{:S(2)}, u32[]{:S(2)}) collective-permute-start(bf16[256,512]{1,0:T(8,128)(2,1)S(1)} %collective-permute-done.6), channel_id=1, source_target_pairs={{0,4},{4,8},{8,12},{1,5},{5,9},{9,13},{2,6},{6,10},{10,14},{3,7},{... | collective-permute-start | bytes 786440 | tf_op jit(solution)/shard_map/ppermute | solution.py:17
  157.6 22.6 %collective-permute-start.8 = (bf16[256,512]{1,0:T(8,128)(2,1)S(1)}, bf16[256,512]{1,0:T(8,128)(2,1)S(1)}, u32[]{:S(2)}, u32[]{:S(2)}) collective-permute-start(bf16[256,512]{1,0:T(8,128)(2,1)S(1)} %collective-permute-done.7), channel_id=1, source_target_pairs={{0,4},{4,8},{8,12},{1,5},{5,9},{9,13},{2,6},{6,10},{10,14},{3,7},{... | collective-permute-start | bytes 786440 | tf_op jit(solution)/shard_map/ppermute | solution.py:17
  180.4 1.4 copy-start.12
  181.8 4.7 copy-start.28
  206.5 35.0 %copy-start.4 = (bf16[64,4096]{1,0:T(8,128)(2,1)S(1)}, bf16[64,4096]{1,0:T(8,128)(2,1)}, u32[]{:S(2)}) copy-start(bf16[64,4096]{1,0:T(8,128)(2,1)} %param.18) | copy-start | bytes 1572868
  206.6 37.1 %copy-start.14 = (f32[4096]{0:T(1024)S(1)}, f32[4096]{0:T(1024)}, u32[]{:S(2)}) copy-start(f32[4096]{0:T(1024)} %param.27) | copy-start | bytes 49156
  206.6 38.1 %copy-start.25 = (s32[1024]{0:T(1024)S(1)}, s32[1024]{0:T(1024)}, u32[]{:S(2)}) copy-start(s32[1024]{0:T(1024)} %param.26) | copy-start | bytes 12292
  206.6 38.2 %copy-start.24 = (f32[4,1024]{1,0:T(4,128)S(1)}, f32[4,1024]{1,0:T(4,128)}, u32[]{:S(2)}) copy-start(f32[4,1024]{1,0:T(4,128)} %param.21) | copy-start | bytes 49156
  206.6 186.1 %all-gather.8.cloned.1.call-start = ((), (), s32[]{:S(2)}) async-start(), calls=%async_computation.4 | async-start | bytes 10485760 | tf_op jit(solution)/shard_map/all_gather | solution.py:104
  207.3 208.2 %all-gather.6.cloned.1.call-start = ((), (), s32[]{:S(2)}) async-start(), calls=%async_computation.3 | async-start | bytes 2621440 | tf_op jit(solution)/shard_map/all_gather | solution.py:100
  242.9 0.8 copy-start.2
  421.9 4.7 collective-permute-start.9
  427.4 1.7 copy-start.5
  429.1 1.7 copy-start.26
  429.1 1.7 copy-start.27
  504.4 7.2 %copy-start.11 = (f32[3,1024]{1,0:T(4,128)S(1)}, f32[3,1024]{1,0:T(4,128)}, u32[]{:S(2)}) copy-start(f32[3,1024]{1,0:T(4,128)} %slice.341) | copy-start | bytes 36868
  504.4 7.2 %copy-start.23 = (f32[1,1024]{1,0:T(1,128)S(1)}, f32[1,1024]{1,0:T(1,128)}, u32[]{:S(2)}) copy-start(f32[1,1024]{1,0:T(1,128)} %slice.407) | copy-start | bytes 12292
  504.4 7.3 %copy-start.22 = (f32[1,1024]{1,0:T(1,128)S(1)}, f32[1,1024]{1,0:T(1,128)}, u32[]{:S(2)}) copy-start(f32[1,1024]{1,0:T(1,128)} %slice.381) | copy-start | bytes 12292
  504.4 7.4 %copy-start.9 = (f32[7,1024]{1,0:T(8,128)S(1)}, f32[7,1024]{1,0:T(8,128)}, u32[]{:S(2)}) copy-start(f32[7,1024]{1,0:T(8,128)} %slice.318) | copy-start | bytes 86020
  504.4 7.4 %copy-start.10 = (f32[7,1024]{1,0:T(8,128)S(1)}, f32[7,1024]{1,0:T(8,128)}, u32[]{:S(2)}) copy-start(f32[7,1024]{1,0:T(8,128)} %slice.343) | copy-start | bytes 86020
  504.4 8.9 %copy-start.7 = (f32[15,1024]{1,0:T(8,128)S(1)}, f32[15,1024]{1,0:T(8,128)}, u32[]{:S(2)}) copy-start(f32[15,1024]{1,0:T(8,128)} %slice.312) | copy-start | bytes 184324
  504.4 8.9 %copy-start.8 = (f32[15,1024]{1,0:T(8,128)S(1)}, f32[15,1024]{1,0:T(8,128)}, u32[]{:S(2)}) copy-start(f32[15,1024]{1,0:T(8,128)} %slice.345) | copy-start | bytes 184324
  507.5 6.8 %copy-start.6 = (f32[31,1024]{1,0:T(8,128)S(1)}, f32[31,1024]{1,0:T(8,128)}, u32[]{:S(2)}) copy-start(f32[31,1024]{1,0:T(8,128)} %slice.347) | copy-start | bytes 380932
  508.1 5.3 copy-start.21
  511.8 2.6 copy-start.20
  513.4 1.2 copy-start.19
  514.3 1.0 copy-start.3
  514.5 0.9 copy-start.18
  515.4 2.9 copy-start.17
  518.6 2.3 copy-start.16
  520.9 3.0 copy-start.15
  521.1 6.6 %copy-start.1 = (f32[256,1024]{1,0:T(8,128)S(1)}, f32[256,1024]{1,0:T(8,128)}, u32[]{:S(2)}) copy-start(f32[256,1024]{1,0:T(8,128)} %pad.114) | copy-start | bytes 3145732
  528.5 5.5 collective-permute-start
  534.0 5.5 collective-permute-start
  539.5 5.5 collective-permute-start
Sparse Core Ops, SparseCore 0:
  9.6 189.8 all-gather.3
  206.7 34.7 reduce-scatter.1
  243.1 149.6 all-gather.7
  394.7 20.7 all-gather.5
where the time goes:
time: 557 us; the launch traced here: 554 us
  waiting for transfers between devices  295 us (53%)
  starting transfers between devices  102 us (18%)
  local copies, waits for them, and re-layouts  77.2 us (14%)
  other arithmetic  32.9 us (6%)
  matrix products  24.8 us (4%)
  between operations  14.7 us (3%)
  blocking collectives  7.43 us (1%)
    all_gather x1, waiting for transfers between devices, local(): lax.all_gather(lru_weight, 'ctx', axis=0, tiled=True)  148 us
    ppermute x12, starting transfers between devices, shifted_2(): lax.ppermute(value, axis, [(source, source + steps) for source in range(i...  102 us
    ppermute x12, waiting for transfers between devices, shifted_2(): lax.ppermute(value, axis, [(source, source + steps) for source in range(i...  82.1 us
    slice x52, local copies, waits for them, and re-layouts, local(): lax.associative_scan(chain_link, (keep_factor, driven), axis=0)  61 us
    reduce_scatter x1, waiting for transfers between devices, local(): lax.psum_scatter(head_part.astype(jnp.bfloat16), 'mp', scatter_dimension=...  33.9 us
    all_gather x1, waiting for transfers between devices, local(): lax.all_gather(rms_scaled(resid_out, norm_gain), 'mp', axis=0, tiled=True)  22.8 us
    add x13, other arithmetic, chain_link(): return (former[0] * latter[0], latter[0] * former[1] + latter[1])  13.8 us
  transfers between devices with their start and end apart: 16, of which 16 were waited for; matrix products, arithmetic and copies ran while one was open for 3% of the time, Pallas kernels for 0%

commit v1 on v0

--- a/solution.py
+++ b/solution.py
@@ -9,6 +9,22 @@
 CONV = 4
 LEVELS = 16
 BW = 256
+
+
+def ring_gather(x, axis, dim):
+    ways, here, step = (lax.axis_size(axis), lax.axis_index(axis), x.shape[dim])
+    shape = [n * ways if d == dim else n for d, n in enumerate(x.shape)]
+    full = lax.dynamic_update_slice_in_dim(jnp.zeros(shape, x.dtype), x, here * step, axis=dim)
+    going_up = going_down = x
+    for far in range(1, ways // 2 + 1):
+        going_up = lax.ppermute(going_up, axis, [(d, (d + 1) % ways) for d in range(ways)])
+        full = lax.dynamic_update_slice_in_dim(full, going_up, (here - far) % ways * step, axis=dim)
+        if 2 * far < ways:
+            going_down = lax.ppermute(going_down, axis, [(d, (d - 1) % ways) for d in range(ways)])
+            full = lax.dynamic_update_slice_in_dim(
+                full, going_down, (here + far) % ways * step, axis=dim
+            )
+    return full
 
 
 def shifted_2(value, axis, steps):
@@ -100,9 +116,7 @@
     normed = lax.all_gather(rms_scaled(resid_out, norm_gain), "mp", axis=0, tiled=True)
     channels = lru_weight.shape[1]
     lru_in = jnp.dot(
-        normed,
-        lax.all_gather(lru_weight, "ctx", axis=0, tiled=True),
-        preferred_element_type=jnp.float32,
+        normed, ring_gather(lru_weight, "ctx", 0), preferred_element_type=jnp.float32
     ).astype(jnp.bfloat16)
     rim_rows = shifted_2(lru_in[rows_here - (CONV - 1) :], "ctx", 1)
     extended = jnp.concatenate([rim_rows, lru_in], axis=0)

time: 557 us -> 491 us (0.88)
  waiting for transfers between devices: 295 us -> 208 us
  local copies, waits for them, and re-layouts: 77.2 us -> 92.8 us
    all_gather x1 -> x0, waiting for transfers between devices: 148 us -> none  [local(): lax.all_gather(lru_weight, 'ctx', axis=0, tiled=True)]
    ppermute x0 -> x3, waiting for transfers between devices: none -> 86.8 us  [the longest x2 51.1 us: ring_gather(): lax.ppermute(going_up, axis, [(d, (d + 1) % ways) for d in range(ways)])]
    all_gather x1, waiting for transfers between devices: 22.8 us -> 0.01 us  [local(): lax.all_gather(rms_scaled(resid_out, norm_gain), 'mp', axis=0, tiled=True)]
    dynamic_update_slice x0 -> x4, local copies, waits for them, and re-layouts: none -> 10.9 us  [the longest x2 6.27 us: ring_gather(): lax.dynamic_update_slice_in_dim(full, going_up, (here - far) % ways * ste...]
    ppermute x0 -> x3, starting transfers between devices: none -> 6.32 us  [the longest x1 3.4 us: ring_gather(): lax.ppermute(going_down, axis, [(d, (d - 1) % ways) for d in range(ways)])]
  transfers between devices with their start and end apart: 16 -> 18, of which waited for: 16 -> 17; matrix products, arithmetic and copies ran while one was open for 3% -> 6% of each run, Pallas kernels for 0% -> 0%
where the time goes in v1:
time: 491 us; the launch traced here: 488 us
  waiting for transfers between devices  208 us (42%)
  starting transfers between devices  107 us (22%)
  local copies, waits for them, and re-layouts  92.8 us (19%)
  other arithmetic  32.9 us (7%)
  matrix products  25 us (5%)
  between operations  14.7 us (3%)
  blocking collectives  7.43 us (2%)
    ppermute x12, starting transfers between devices, shifted_2(): lax.ppermute(value, axis, [(source, source + steps) for source in range(i...  100 us
    ppermute x12, waiting for transfers between devices, shifted_2(): lax.ppermute(value, axis, [(source, source + steps) for source in range(i...  82.1 us
    slice x52, local copies, waits for them, and re-layouts, local(): lax.associative_scan(chain_link, (keep_factor, driven), axis=0)  61.2 us
    ppermute x2, waiting for transfers between devices, ring_gather(): lax.ppermute(going_up, axis, [(d, (d + 1) % ways) for d in range(ways)])  51.1 us
    ppermute x1, waiting for transfers between devices, ring_gather(): lax.ppermute(going_down, axis, [(d, (d - 1) % ways) for d in range(ways)])  35.7 us
    reduce_scatter x1, waiting for transfers between devices, local(): lax.psum_scatter(head_part.astype(jnp.bfloat16), 'mp', scatter_dimension=...  32 us
    add x13, other arithmetic, chain_link(): return (former[0] * latter[0], latter[0] * former[1] + latter[1])  13.9 us
    pad x28, local copies, waits for them, and re-layouts, local(): lax.associative_scan(chain_link, (keep_factor, driven), axis=0)  10.4 us
  transfers between devices with their start and end apart: 18, of which 17 were waited for; matrix products, arithmetic and copies ran while one was open for 6% of the time, Pallas kernels for 0%

profile of v1, /device:TPU:0, one launch (start us, length us, event | category | flops | bytes accessed | tf_op | source)
XLA Modules:
  0.0 488.1 jit_solution(3460600048332218284)
XLA Ops:
  8.0 7.4 %all_gather.9 = bf16[256,512]{1,0:T(8,128)(2,1)S(1)} all-gather(bf16[64,512]{1,0:T(8,128)(2,1)} %param.16), channel_id=1, replica_groups=mesh['groups'=2,'ctx'=4,'mp'=4] {'mp'}, dimensions={0}, use_global_device_ids=true | all-gather | bytes 327680 | tf_op jit(solution)/shard_map/all_gather | solution.py:88
  15.4 3.5 collective-permute-start.1
  18.9 9.3 %collective-permute-done.1 = bf16[256,512]{1,0:T(8,128)(2,1)S(1)} collective-permute-done((bf16[256,512]{1,0:T(8,128)(2,1)S(1)}, bf16[256,512]{1,0:T(8,128)(2,1)S(1)}, u32[]{:S(2)}, u32[]{:S(2)}) %collective-permute-start.1) | collective-permute-done | bytes 262176 | tf_op jit(solution)/shard_map/ppermute | solution.py:33
  28.3 8.5 %collective-permute-start.2 = (bf16[256,512]{1,0:T(8,128)(2,1)S(1)}, bf16[256,512]{1,0:T(8,128)(2,1)S(1)}, u32[]{:S(2)}, u32[]{:S(2)}) collective-permute-start(bf16[256,512]{1,0:T(8,128)(2,1)S(1)} %collective-permute-done.1), channel_id=1, source_target_pairs={{0,4},{4,8},{8,12},{1,5},{5,9},{9,13},{2,6},{6,10},{10,14},{3,7},{... | collective-permute-start | bytes 786440 | tf_op jit(solution)/shard_map/ppermute | solution.py:33
  36.8 11.2 %collective-permute-done.2 = bf16[256,512]{1,0:T(8,128)(2,1)S(1)} collective-permute-done((bf16[256,512]{1,0:T(8,128)(2,1)S(1)}, bf16[256,512]{1,0:T(8,128)(2,1)S(1)}, u32[]{:S(2)}, u32[]{:S(2)}) %collective-permute-start.2) | collective-permute-done | bytes 262176 | tf_op jit(solution)/shard_map/ppermute | solution.py:33
  48.0 13.6 %collective-permute-start.3 = (bf16[256,512]{1,0:T(8,128)(2,1)S(1)}, bf16[256,512]{1,0:T(8,128)(2,1)S(1)}, u32[]{:S(2)}, u32[]{:S(2)}) collective-permute-start(bf16[256,512]{1,0:T(8,128)(2,1)S(1)} %collective-permute-done.2), channel_id=1, source_target_pairs={{0,4},{4,8},{8,12},{1,5},{5,9},{9,13},{2,6},{6,10},{10,14},{3,7},{... | collective-permute-start | bytes 786440 | tf_op jit(solution)/shard_map/ppermute | solution.py:33
  61.6 10.2 %collective-permute-done.3 = bf16[256,512]{1,0:T(8,128)(2,1)S(1)} collective-permute-done((bf16[256,512]{1,0:T(8,128)(2,1)S(1)}, bf16[256,512]{1,0:T(8,128)(2,1)S(1)}, u32[]{:S(2)}, u32[]{:S(2)}) %collective-permute-start.3) | collective-permute-done | bytes 262176 | tf_op jit(solution)/shard_map/ppermute | solution.py:33
  71.8 12.3 %collective-permute-start.4 = (bf16[256,512]{1,0:T(8,128)(2,1)S(1)}, bf16[256,512]{1,0:T(8,128)(2,1)S(1)}, u32[]{:S(2)}, u32[]{:S(2)}) collective-permute-start(bf16[256,512]{1,0:T(8,128)(2,1)S(1)} %collective-permute-done.3), channel_id=1, source_target_pairs={{0,4},{4,8},{8,12},{1,5},{5,9},{9,13},{2,6},{6,10},{10,14},{3,7},{... | collective-permute-start | bytes 786440 | tf_op jit(solution)/shard_map/ppermute | solution.py:33
  84.1 9.6 %collective-permute-done.4 = bf16[256,512]{1,0:T(8,128)(2,1)S(1)} collective-permute-done((bf16[256,512]{1,0:T(8,128)(2,1)S(1)}, bf16[256,512]{1,0:T(8,128)(2,1)S(1)}, u32[]{:S(2)}, u32[]{:S(2)}) %collective-permute-start.4) | collective-permute-done | bytes 262176 | tf_op jit(solution)/shard_map/ppermute | solution.py:33
  93.7 11.3 %collective-permute-start.5 = (bf16[256,512]{1,0:T(8,128)(2,1)S(1)}, bf16[256,512]{1,0:T(8,128)(2,1)S(1)}, u32[]{:S(2)}, u32[]{:S(2)}) collective-permute-start(bf16[256,512]{1,0:T(8,128)(2,1)S(1)} %collective-permute-done.4), channel_id=1, source_target_pairs={{0,4},{4,8},{8,12},{1,5},{5,9},{9,13},{2,6},{6,10},{10,14},{3,7},{... | collective-permute-start | bytes 786440 | tf_op jit(solution)/shard_map/ppermute | solution.py:33
  105.0 9.7 %collective-permute-done.5 = bf16[256,512]{1,0:T(8,128)(2,1)S(1)} collective-permute-done((bf16[256,512]{1,0:T(8,128)(2,1)S(1)}, bf16[256,512]{1,0:T(8,128)(2,1)S(1)}, u32[]{:S(2)}, u32[]{:S(2)}) %collective-permute-start.5) | collective-permute-done | bytes 262176 | tf_op jit(solution)/shard_map/ppermute | solution.py:33
  114.6 13.8 %collective-permute-start.6 = (bf16[256,512]{1,0:T(8,128)(2,1)S(1)}, bf16[256,512]{1,0:T(8,128)(2,1)S(1)}, u32[]{:S(2)}, u32[]{:S(2)}) collective-permute-start(bf16[256,512]{1,0:T(8,128)(2,1)S(1)} %collective-permute-done.5), channel_id=1, source_target_pairs={{0,4},{4,8},{8,12},{1,5},{5,9},{9,13},{2,6},{6,10},{10,14},{3,7},{... | collective-permute-start | bytes 786440 | tf_op jit(solution)/shard_map/ppermute | solution.py:33
  128.7 9.4 %collective-permute-done.6 = bf16[256,512]{1,0:T(8,128)(2,1)S(1)} collective-permute-done((bf16[256,512]{1,0:T(8,128)(2,1)S(1)}, bf16[256,512]{1,0:T(8,128)(2,1)S(1)}, u32[]{:S(2)}, u32[]{:S(2)}) %collective-permute-start.6) | collective-permute-done | bytes 262176 | tf_op jit(solution)/shard_map/ppermute | solution.py:33
  138.1 9.9 %collective-permute-start.7 = (bf16[256,512]{1,0:T(8,128)(2,1)S(1)}, bf16[256,512]{1,0:T(8,128)(2,1)S(1)}, u32[]{:S(2)}, u32[]{:S(2)}) collective-permute-start(bf16[256,512]{1,0:T(8,128)(2,1)S(1)} %collective-permute-done.6), channel_id=1, source_target_pairs={{0,4},{4,8},{8,12},{1,5},{5,9},{9,13},{2,6},{6,10},{10,14},{3,7},{... | collective-permute-start | bytes 786440 | tf_op jit(solution)/shard_map/ppermute | solution.py:33
  148.1 9.5 %collective-permute-done.7 = bf16[256,512]{1,0:T(8,128)(2,1)S(1)} collective-permute-done((bf16[256,512]{1,0:T(8,128)(2,1)S(1)}, bf16[256,512]{1,0:T(8,128)(2,1)S(1)}, u32[]{:S(2)}, u32[]{:S(2)}) %collective-permute-start.7) | collective-permute-done | bytes 262176 | tf_op jit(solution)/shard_map/ppermute | solution.py:33
  157.6 13.0 %collective-permute-start.8 = (bf16[256,512]{1,0:T(8,128)(2,1)S(1)}, bf16[256,512]{1,0:T(8,128)(2,1)S(1)}, u32[]{:S(2)}, u32[]{:S(2)}) collective-permute-start(bf16[256,512]{1,0:T(8,128)(2,1)S(1)} %collective-permute-done.7), channel_id=1, source_target_pairs={{0,4},{4,8},{8,12},{1,5},{5,9},{9,13},{2,6},{6,10},{10,14},{3,7},{... | collective-permute-start | bytes 786440 | tf_op jit(solution)/shard_map/ppermute | solution.py:33
  170.6 1.6 fusion.7
  172.2 8.0 %collective-permute-done.8 = bf16[256,512]{1,0:T(8,128)(2,1)S(1)} collective-permute-done((bf16[256,512]{1,0:T(8,128)(2,1)S(1)}, bf16[256,512]{1,0:T(8,128)(2,1)S(1)}, u32[]{:S(2)}, u32[]{:S(2)}) %collective-permute-start.8) | collective-permute-done | bytes 262176 | tf_op jit(solution)/shard_map/ppermute | solution.py:33
  181.8 4.7 fusion.53
  186.5 6.0 %fusion.8 = bf16[256,4,256]{2,0,1:T(8,128)(2,1)S(1)} fusion(f32[4,256]{1,0:T(4,128)S(1)} %fusion.53, bf16[2304,512]{1,0:T(8,128)(2,1)} %copy-done.13, pred[256,2304]{0,1:T(8,128)(4,1)S(1)} %fusion.7, bf16[32,4,8,256]{3,2,1,0:T(8,128)(2,1)S(1)} %bitcast.79), kind=kOutput, calls=%fused_computation.17 | convolution fusion | flops 2427981056 | bytes 4001792 | tf_op jit(solution)/shard_map/htk,kd->thd/dot_general | solution.py:64
  192.5 6.9 %all-gather.3.cloned.1.call-done = bf16[1024,4096]{1,0:T(8,128)(2,1)} async-done(((bf16[1024,1024]{1,0:T(8,128)(2,1)}), bf16[1024,4096]{1,0:T(8,128)(2,1)}) %all-gather.3.cloned.1.call-update) | async-done | bytes 8388624 | tf_op jit(solution)/shard_map/all_gather | solution.py:109
  199.5 7.2 %convolution_convert_fusion = bf16[256,4096]{1,0:T(8,128)(2,1)} fusion(bf16[256,1024]{0,1:T(8,128)(2,1)S(1)} %bitcast.71, bf16[1024,4096]{1,0:T(8,128)(2,1)} %all-gather.3.cloned.1.call-done), kind=kOutput, calls=%fused_computation.6 | convolution fusion | flops 2148532224 | bytes 11010048 | tf_op jit(solution)/shard_map/dot_general | solution.py:107
  206.8 2.9 collective-permute-start.9
  209.7 32.0 %reduce-scatter.2.cloned.1.call-done = bf16[64,4096]{1,0:T(8,128)(2,1)} async-done(((bf16[256,4096]{1,0:T(8,128)(2,1)}), bf16[64,4096]{1,0:T(8,128)(2,1)}) %reduce-scatter.2.cloned.1.call-update) | async-done | bytes 524304 | tf_op jit(solution)/shard_map/reduce_scatter | solution.py:112
  244.8 3.4 collective-permute-start.10
  248.2 11.4 %collective-permute-done.9 = bf16[1024,1024]{1,0:T(8,128)(2,1)} collective-permute-done((bf16[1024,1024]{1,0:T(8,128)(2,1)S(1)}, bf16[1024,1024]{1,0:T(8,128)(2,1)}, u32[]{:S(2)}, u32[]{:S(2)}) %collective-permute-start.9) | collective-permute-done | bytes 2097184 | tf_op jit(solution)/shard_map/ppermute | solution.py:20
  259.7 4.4 broadcast_in_dim.103
  264.1 1.5 constant_dynamic-update-slice_fusion.12
  265.7 3.1 constant_dynamic-update-slice_fusion.11
  268.8 35.7 %collective-permute-done.10 = bf16[1024,1024]{1,0:T(8,128)(2,1)} collective-permute-done((bf16[1024,1024]{1,0:T(8,128)(2,1)S(1)}, bf16[1024,1024]{1,0:T(8,128)(2,1)}, u32[]{:S(2)}, u32[]{:S(2)}) %collective-permute-start.10) | collective-permute-done | bytes 2097184 | tf_op jit(solution)/shard_map/ppermute | solution.py:23
  304.5 3.1 constant_dynamic-update-slice_fusion.10
  307.6 39.7 %collective-permute-done.11 = bf16[1024,1024]{1,0:T(8,128)(2,1)} collective-permute-done((bf16[1024,1024]{1,0:T(8,128)(2,1)}, bf16[1024,1024]{1,0:T(8,128)(2,1)}, u32[]{:S(2)}, u32[]{:S(2)}) %collective-permute-start.11) | collective-permute-done | bytes 2097184 | tf_op jit(solution)/shard_map/ppermute | solution.py:20
  347.3 3.1 constant_dynamic-update-slice_fusion.9
  350.4 6.3 %convolution_convert_fusion.1 = bf16[256,1024]{1,0:T(8,128)(2,1)S(1)} fusion(bf16[256,4096]{1,0:T(8,128)(2,1)} %all-gather.5.cloned.1.call-done, bf16[4096,1024]{1,0:T(8,128)(2,1)} %constant_dynamic-update-slice_fusion.9), kind=kOutput, calls=%fused_computation.18 | convolution fusion | flops 2147745792 | bytes 11010048 | tf_op jit(solution)/shard_map/dot_general | solution.py:118
  356.8 1.9 collective-permute-start.12
  364.2 2.8 convert_multiply_fusion.2
  367.0 1.5 slice.296
  370.0 1.5 slice.295
  372.9 2.5 multiply_add_fusion.1
  375.4 1.7 slice.302
  377.1 1.7 slice.303
  380.3 1.9 multiply_add_fusion.2
  383.7 1.6 slice.307
  385.3 1.6 slice.311
  386.9 1.8 multiply_add_fusion.3
  390.0 1.5 slice.313
  391.5 1.5 slice.317
  393.0 1.6 multiply_add_fusion.4
  399.0 1.5 slice.323
  420.9 1.5 slice.318
  422.3 1.5 slice.343
  426.5 1.5 slice.312
  434.4 1.7 slice.349
  438.1 1.5 slice.294
  439.7 1.5 slice.351
  449.4 2.7 pad.114
  452.3 2.3 fusion.24
  454.9 2.7 pad.130
  458.7 2.7 pad.129
  462.2 16.5 %while.10 = (s32[]{:T(128)}, f32[1024]{0:T(1024)S(1)}, f32[1024]{0:T(1024)S(1)}, f32[1024]{0:T(1024)S(1)}, s32[]{:T(128)}) while((s32[]{:T(128)}, f32[1024]{0:T(1024)S(1)}, f32[1024]{0:T(1024)S(1)}, f32[1024]{0:T(1024)S(1)}, s32[]{:T(128)}) %tuple.61), condition=%wide.region_6.7_spmd, body=%wide.region_5.6_spmd.sunk | while | flops 2050 | bytes 32869 | solution.py:163
  462.3 4.2 collective-permute-start
  467.8 4.2 collective-permute-start
  473.3 4.2 collective-permute-start
  478.8 2.8 add_convert_fusion
  (205 shorter events, 68.2 us)
Async XLA Ops:
  7.2 353.7 %copy-start = (bf16[4,256,256]{2,1,0:T(8,128)(2,1)S(1)}, bf16[4,256,256]{2,1,0:T(8,128)(2,1)}, u32[]{:S(2)}) copy-start(bf16[4,256,256]{2,1,0:T(8,128)(2,1)} %param.22) | copy-start | bytes 1572868
  7.2 121.3 %copy-start.14 = (s32[1024]{0:T(1024)S(1)}, s32[1024]{0:T(1024)}, u32[]{:S(2)}) copy-start(s32[1024]{0:T(1024)} %param.17) | copy-start | bytes 12292
  7.2 192.3 %all-gather.3.cloned.1.call-start = ((), (), s32[]{:S(2)}) async-start(), calls=%async_computation.1 | async-start | bytes 10485760 | tf_op jit(solution)/shard_map/all_gather | solution.py:109
  7.9 233.8 %reduce-scatter.2.cloned.1.call-start = ((), (), s32[]{:S(2)}) async-start(), calls=%async_computation.2 | async-start | bytes 2621440 | tf_op jit(solution)/shard_map/reduce_scatter | solution.py:112
  15.4 12.9 %collective-permute-start.1 = (bf16[256,512]{1,0:T(8,128)(2,1)S(1)}, bf16[256,512]{1,0:T(8,128)(2,1)S(1)}, u32[]{:S(2)}, u32[]{:S(2)}) collective-permute-start(bf16[256,512]{1,0:T(8,128)(2,1)S(1)} %all_gather.9), channel_id=1, source_target_pairs={{0,4},{4,8},{8,12},{1,5},{5,9},{9,13},{2,6},{6,10},{10,14},{3,7},{... | collective-permute-start | bytes 786440 | tf_op jit(solution)/shard_map/ppermute | solution.py:33
  28.3 19.7 %collective-permute-start.2 = (bf16[256,512]{1,0:T(8,128)(2,1)S(1)}, bf16[256,512]{1,0:T(8,128)(2,1)S(1)}, u32[]{:S(2)}, u32[]{:S(2)}) collective-permute-start(bf16[256,512]{1,0:T(8,128)(2,1)S(1)} %collective-permute-done.1), channel_id=1, source_target_pairs={{0,4},{4,8},{8,12},{1,5},{5,9},{9,13},{2,6},{6,10},{10,14},{3,7},{... | collective-permute-start | bytes 786440 | tf_op jit(solution)/shard_map/ppermute | solution.py:33
  48.0 23.8 %collective-permute-start.3 = (bf16[256,512]{1,0:T(8,128)(2,1)S(1)}, bf16[256,512]{1,0:T(8,128)(2,1)S(1)}, u32[]{:S(2)}, u32[]{:S(2)}) collective-permute-start(bf16[256,512]{1,0:T(8,128)(2,1)S(1)} %collective-permute-done.2), channel_id=1, source_target_pairs={{0,4},{4,8},{8,12},{1,5},{5,9},{9,13},{2,6},{6,10},{10,14},{3,7},{... | collective-permute-start | bytes 786440 | tf_op jit(solution)/shard_map/ppermute | solution.py:33
  71.8 21.9 %collective-permute-start.4 = (bf16[256,512]{1,0:T(8,128)(2,1)S(1)}, bf16[256,512]{1,0:T(8,128)(2,1)S(1)}, u32[]{:S(2)}, u32[]{:S(2)}) collective-permute-start(bf16[256,512]{1,0:T(8,128)(2,1)S(1)} %collective-permute-done.3), channel_id=1, source_target_pairs={{0,4},{4,8},{8,12},{1,5},{5,9},{9,13},{2,6},{6,10},{10,14},{3,7},{... | collective-permute-start | bytes 786440 | tf_op jit(solution)/shard_map/ppermute | solution.py:33
  93.7 21.0 %collective-permute-start.5 = (bf16[256,512]{1,0:T(8,128)(2,1)S(1)}, bf16[256,512]{1,0:T(8,128)(2,1)S(1)}, u32[]{:S(2)}, u32[]{:S(2)}) collective-permute-start(bf16[256,512]{1,0:T(8,128)(2,1)S(1)} %collective-permute-done.4), channel_id=1, source_target_pairs={{0,4},{4,8},{8,12},{1,5},{5,9},{9,13},{2,6},{6,10},{10,14},{3,7},{... | collective-permute-start | bytes 786440 | tf_op jit(solution)/shard_map/ppermute | solution.py:33
  114.6 23.4 %collective-permute-start.6 = (bf16[256,512]{1,0:T(8,128)(2,1)S(1)}, bf16[256,512]{1,0:T(8,128)(2,1)S(1)}, u32[]{:S(2)}, u32[]{:S(2)}) collective-permute-start(bf16[256,512]{1,0:T(8,128)(2,1)S(1)} %collective-permute-done.5), channel_id=1, source_target_pairs={{0,4},{4,8},{8,12},{1,5},{5,9},{9,13},{2,6},{6,10},{10,14},{3,7},{... | collective-permute-start | bytes 786440 | tf_op jit(solution)/shard_map/ppermute | solution.py:33
  138.1 19.5 %collective-permute-start.7 = (bf16[256,512]{1,0:T(8,128)(2,1)S(1)}, bf16[256,512]{1,0:T(8,128)(2,1)S(1)}, u32[]{:S(2)}, u32[]{:S(2)}) collective-permute-start(bf16[256,512]{1,0:T(8,128)(2,1)S(1)} %collective-permute-done.6), channel_id=1, source_target_pairs={{0,4},{4,8},{8,12},{1,5},{5,9},{9,13},{2,6},{6,10},{10,14},{3,7},{... | collective-permute-start | bytes 786440 | tf_op jit(solution)/shard_map/ppermute | solution.py:33
  157.6 22.6 %collective-permute-start.8 = (bf16[256,512]{1,0:T(8,128)(2,1)S(1)}, bf16[256,512]{1,0:T(8,128)(2,1)S(1)}, u32[]{:S(2)}, u32[]{:S(2)}) collective-permute-start(bf16[256,512]{1,0:T(8,128)(2,1)S(1)} %collective-permute-done.7), channel_id=1, source_target_pairs={{0,4},{4,8},{8,12},{1,5},{5,9},{9,13},{2,6},{6,10},{10,14},{3,7},{... | collective-permute-start | bytes 786440 | tf_op jit(solution)/shard_map/ppermute | solution.py:33
  180.4 1.4 copy-start.13
  181.8 4.7 copy-start.29
  199.5 7.3 %copy-start.2 = (bf16[1024,1024]{1,0:T(8,128)(2,1)S(1)}, bf16[1024,1024]{1,0:T(8,128)(2,1)}, u32[]{:S(2)}) copy-start(bf16[1024,1024]{1,0:T(8,128)(2,1)} %param.20) | copy-start | bytes 6291460
  206.7 35.0 %copy-start.5 = (bf16[64,4096]{1,0:T(8,128)(2,1)S(1)}, bf16[64,4096]{1,0:T(8,128)(2,1)}, u32[]{:S(2)}) copy-start(bf16[64,4096]{1,0:T(8,128)(2,1)} %param.18) | copy-start | bytes 1572868
  206.7 37.1 %copy-start.15 = (f32[4096]{0:T(1024)S(1)}, f32[4096]{0:T(1024)}, u32[]{:S(2)}) copy-start(f32[4096]{0:T(1024)} %param.27) | copy-start | bytes 49156
  206.7 52.9 %copy-start.26 = (s32[1024]{0:T(1024)S(1)}, s32[1024]{0:T(1024)}, u32[]{:S(2)}) copy-start(s32[1024]{0:T(1024)} %param.26) | copy-start | bytes 12292
  206.7 143.7 %all-gather.5.cloned.1.call-start = ((), (), s32[]{:S(2)}) async-start(), calls=%async_computation.3 | async-start | bytes 2621440 | tf_op jit(solution)/shard_map/all_gather | solution.py:116
  206.8 52.8 %collective-permute-start.9 = (bf16[1024,1024]{1,0:T(8,128)(2,1)S(1)}, bf16[1024,1024]{1,0:T(8,128)(2,1)}, u32[]{:S(2)}, u32[]{:S(2)}) collective-permute-start(bf16[1024,1024]{1,0:T(8,128)(2,1)S(1)} %copy-done.2), channel_id=1, source_target_pairs={{0,4},{4,8},{8,12},{12,0},{1,5},{5,9},{9,13},{13,1},{2,6},{6,10},{... | collective-permute-start | bytes 6291464 | tf_op jit(solution)/shard_map/ppermute | solution.py:20
  243.0 0.8 copy-start.3
  244.8 59.6 %collective-permute-start.10 = (bf16[1024,1024]{1,0:T(8,128)(2,1)S(1)}, bf16[1024,1024]{1,0:T(8,128)(2,1)}, u32[]{:S(2)}, u32[]{:S(2)}) collective-permute-start(bf16[1024,1024]{1,0:T(8,128)(2,1)S(1)} %copy-done.2), channel_id=1, source_target_pairs={{0,12},{4,0},{8,4},{12,8},{1,13},{5,1},{9,5},{13,9},{2,14},{6,2},{... | collective-permute-start | bytes 6291464 | tf_op jit(solution)/shard_map/ppermute | solution.py:23
  259.6 87.7 %collective-permute-start.11 = (bf16[1024,1024]{1,0:T(8,128)(2,1)}, bf16[1024,1024]{1,0:T(8,128)(2,1)}, u32[]{:S(2)}, u32[]{:S(2)}) collective-permute-start(bf16[1024,1024]{1,0:T(8,128)(2,1)} %collective-permute-done.9), channel_id=1, source_target_pairs={{0,4},{4,8},{8,12},{12,0},{1,5},{5,9},{9,13},{13,1},{2,6},{6,10},{... | collective-permute-start | bytes 6291464 | tf_op jit(solution)/shard_map/ppermute | solution.py:20
  264.1 1.5 copy-start.25
  356.8 3.3 collective-permute-start.12
  360.8 1.7 copy-start.6
  362.5 1.7 copy-start.27
  362.5 1.7 copy-start.28
  438.1 7.2 %copy-start.12 = (f32[3,1024]{1,0:T(4,128)S(1)}, f32[3,1024]{1,0:T(4,128)}, u32[]{:S(2)}) copy-start(f32[3,1024]{1,0:T(4,128)} %slice.341) | copy-start | bytes 36868
  438.1 7.3 %copy-start.24 = (f32[1,1024]{1,0:T(1,128)S(1)}, f32[1,1024]{1,0:T(1,128)}, u32[]{:S(2)}) copy-start(f32[1,1024]{1,0:T(1,128)} %slice.407) | copy-start | bytes 12292
  438.1 7.3 %copy-start.23 = (f32[1,1024]{1,0:T(1,128)S(1)}, f32[1,1024]{1,0:T(1,128)}, u32[]{:S(2)}) copy-start(f32[1,1024]{1,0:T(1,128)} %slice.381) | copy-start | bytes 12292
  438.1 7.4 %copy-start.10 = (f32[7,1024]{1,0:T(8,128)S(1)}, f32[7,1024]{1,0:T(8,128)}, u32[]{:S(2)}) copy-start(f32[7,1024]{1,0:T(8,128)} %slice.318) | copy-start | bytes 86020
  438.1 7.4 %copy-start.11 = (f32[7,1024]{1,0:T(8,128)S(1)}, f32[7,1024]{1,0:T(8,128)}, u32[]{:S(2)}) copy-start(f32[7,1024]{1,0:T(8,128)} %slice.343) | copy-start | bytes 86020
  438.1 9.0 %copy-start.8 = (f32[15,1024]{1,0:T(8,128)S(1)}, f32[15,1024]{1,0:T(8,128)}, u32[]{:S(2)}) copy-start(f32[15,1024]{1,0:T(8,128)} %slice.312) | copy-start | bytes 184324
  438.1 9.0 %copy-start.9 = (f32[15,1024]{1,0:T(8,128)S(1)}, f32[15,1024]{1,0:T(8,128)}, u32[]{:S(2)}) copy-start(f32[15,1024]{1,0:T(8,128)} %slice.345) | copy-start | bytes 184324
  441.2 6.8 %copy-start.7 = (f32[31,1024]{1,0:T(8,128)S(1)}, f32[31,1024]{1,0:T(8,128)}, u32[]{:S(2)}) copy-start(f32[31,1024]{1,0:T(8,128)} %slice.347) | copy-start | bytes 380932
  441.8 5.3 %copy-start.22 = (f32[1,1024]{1,0:T(1,128)S(1)}, f32[1,1024]{1,0:T(1,128)}, u32[]{:S(2)}) copy-start(f32[1,1024]{1,0:T(1,128)} %slice.405) | copy-start | bytes 12292
  445.5 2.6 copy-start.21
  447.1 1.2 copy-start.20
  448.0 1.0 copy-start.4
  448.2 0.9 copy-start.19
  449.1 3.0 copy-start.18
  452.3 2.3 copy-start.17
  454.6 3.0 copy-start.16
  454.8 6.6 %copy-start.1 = (f32[256,1024]{1,0:T(8,128)S(1)}, f32[256,1024]{1,0:T(8,128)}, u32[]{:S(2)}) copy-start(f32[256,1024]{1,0:T(8,128)} %pad.114) | copy-start | bytes 3145732
  462.3 5.5 %collective-permute-start = (f32[1024]{0:T(1024)S(1)}, f32[1024]{0:T(1024)S(1)}, u32[]{:S(2)}, u32[]{:S(2)}) collective-permute-start(f32[1024]{0:T(1024)S(1)} %multiply_add_fusion.9), channel_id=1, source_target_pairs={{0,4},{4,8},{8,12},{1,5},{5,9},{9,13},{2,6},{6,10},{10,14},{3,7},{... | collective-permute-start | bytes 12296 | tf_op jit(solution)/shard_map/while/body/eval_jaxpr/ppermute | solution.py:33
  467.8 5.5 %collective-permute-start = (f32[1024]{0:T(1024)S(1)}, f32[1024]{0:T(1024)S(1)}, u32[]{:S(2)}, u32[]{:S(2)}) collective-permute-start(f32[1024]{0:T(1024)S(1)} %multiply_add_fusion.9), channel_id=1, source_target_pairs={{0,4},{4,8},{8,12},{1,5},{5,9},{9,13},{2,6},{6,10},{10,14},{3,7},{... | collective-permute-start | bytes 12296 | tf_op jit(solution)/shard_map/while/body/eval_jaxpr/ppermute | solution.py:33
  473.3 5.5 %collective-permute-start = (f32[1024]{0:T(1024)S(1)}, f32[1024]{0:T(1024)S(1)}, u32[]{:S(2)}, u32[]{:S(2)}) collective-permute-start(f32[1024]{0:T(1024)S(1)} %multiply_add_fusion.9), channel_id=1, source_target_pairs={{0,4},{4,8},{8,12},{1,5},{5,9},{9,13},{2,6},{6,10},{10,14},{3,7},{... | collective-permute-start | bytes 12296 | tf_op jit(solution)/shard_map/while/body/eval_jaxpr/ppermute | solution.py:33
Sparse Core Ops, SparseCore 0:
  9.6 189.8 all-gather.2
  206.9 34.7 reduce-scatter.1
  245.0 22.5 all-gather.4
